TPU v7x, 32 devices: a whole 2x2x4 slice. The times are simulated.
32 devices in a mesh: groups: 2 (over y), dp: 4 (over z), tensor: 2 (over x), layer: 2 (over core).
Axes of the slice: x: 2, y: 2, z: 4, core: 2. Of those that a mesh axis runs over, the one named last changes fastest.
Arguments:
- train_inputs: bfloat16 [2, 256, 16, 8192], P('layer', ('groups', 'dp'), None, 'tensor'), parts along dimension 1, may hold values from -6 to 6
- train_grads: bfloat16 [2, 256, 16, 8192], P('layer', ('groups', 'dp'), None, 'tensor'), parts along dimension 1, may hold values from -6 to 6
- bench_inputs: bfloat16 [2, 128, 16, 8192], P('layer', ('groups', 'dp'), None, 'tensor'), parts along dimension 1, may hold values from -6 to 6
- bench_grads: bfloat16 [2, 128, 16, 8192], P('layer', ('groups', 'dp'), None, 'tensor'), parts along dimension 1, may hold values from -6 to 6
- answer_mask: int32 [128, 16], P(('groups', 'dp')), parts along dimension 0, may hold values 0 or 1
- factors: bfloat16 [2, 8192, 128], P('layer', 'tensor'), may hold values from -0.0625 to 0.0625
- precond: bfloat16 [2, 4096, 4096], P('layer', None, ('dp', 'tensor')), may hold values from -0.09375 to 0.09375
Outputs:
- scores: float32 [256, 64], P(('groups', 'dp', 'tensor', 'layer')), parts along dimension 0
There are 2 independent parts, one for each index of `groups`. A program takes and returns all parts, laid end to end along the dimension named above; an argument that names none is the same for every part. Nothing has to cross between parts.
All inputs are finite; a program needn't handle non-finite values. No bound on the sum of `answer_mask` on one device may be relied on, other than what follows from the above.
Results may differ from a plain program's by a relative error of at most 0.005.
Values may be sent and summed in bfloat16 or wider, within the bound.
A program may use at most 64 MiB of HBM per device.

v0:
```python
import math

import jax
import jax.numpy as jnp
from jax import lax
from jax.sharding import PartitionSpec as P


def project(inputs_here, grads_here, factor):
    examples, length, shard_width = inputs_here.shape
    factor_width = factor.shape[1] // 2
    in_proj = jnp.dot(
        inputs_here.reshape(examples * length, shard_width),
        factor[:, :factor_width],
        preferred_element_type=jnp.float32,
    )
    out_proj = jnp.dot(
        grads_here.reshape(examples * length, shard_width),
        factor[:, factor_width:],
        preferred_element_type=jnp.float32,
    )
    return jnp.concatenate([in_proj, out_proj], axis=1)


def outer_features(token_rows, examples, length, factor_width):
    grouped = token_rows.reshape(examples, length, 2 * factor_width)
    outer = jnp.einsum(
        "esa,esb->eab",
        grouped[..., factor_width:],
        grouped[..., :factor_width],
        precision=lax.Precision.HIGHEST,
    ) / math.sqrt(length)
    return outer.reshape(examples, factor_width * factor_width).astype(jnp.bfloat16)


def local(train_inputs, train_grads, bench_inputs, bench_grads, answer_mask, factors, precond):
    factor = factors[0]
    factor_width = factor.shape[1] // 2
    length = train_inputs.shape[2]
    masked = bench_grads[0] * answer_mask.astype(jnp.bfloat16)[:, :, None]
    train_rows = project(train_inputs[0], train_grads[0], factor)
    bench_rows = project(bench_inputs[0], masked, factor)
    tensor_count = lax.axis_size("tensor")
    train_each = train_inputs.shape[1] // tensor_count
    bench_each = bench_inputs.shape[1] // tensor_count
    row_width = train_rows.shape[1]
    blocks = jnp.concatenate(
        [
            train_rows.reshape(tensor_count, train_each * length, row_width),
            bench_rows.reshape(tensor_count, bench_each * length, row_width),
        ],
        axis=1,
    ).reshape(-1, row_width)
    share_rows = blocks.shape[0] // tensor_count
    summed = lax.psum(blocks, "tensor")
    own_rows = lax.dynamic_slice_in_dim(
        summed, lax.axis_index("tensor") * share_rows, share_rows, 0
    )
    train_feats = outer_features(own_rows[: train_each * length], train_each, length, factor_width)
    bench_feats = outer_features(own_rows[train_each * length :], bench_each, length, factor_width)
    columns = precond[0]
    pre_cols = jnp.dot(
        lax.all_gather(bench_feats, ("dp", "tensor"), axis=0, tiled=True),
        columns,
        preferred_element_type=jnp.float32,
    ).astype(jnp.bfloat16)
    layer_total = lax.axis_size("layer") * train_inputs.shape[0]
    score_scale = 1.0 / math.sqrt(factor_width * factor_width * layer_total)
    whole_pre = lax.all_gather(pre_cols, ("dp", "tensor"), axis=1, tiled=True)
    partial_value = jnp.einsum(
        "ek,jk->ej", train_feats, whole_pre, preferred_element_type=jnp.float32
    )
    scores = lax.psum_scatter(partial_value, "layer", scatter_dimension=0, tiled=True)
    return scores * score_scale


def solution(mesh):
    placed = (
        P("layer", ("groups", "dp"), None, "tensor"),
        P("layer", ("groups", "dp"), None, "tensor"),
        P("layer", ("groups", "dp"), None, "tensor"),
        P("layer", ("groups", "dp"), None, "tensor"),
        P(("groups", "dp"), None),
        P("layer", "tensor", None),
        P("layer", None, ("dp", "tensor")),
    )
    return jax.shard_map(
        local,
        mesh=mesh,
        in_specs=placed,
        out_specs=P(("groups", "dp", "tensor", "layer"), None),
        check_vma=False,
    )
```

profile of v0, /device:TPU:0, one launch (start us, length us, event | category | flops | bytes accessed | tf_op | source)
XLA Modules:
  0.0 126.8 jit_solution(3071101061029327510)
XLA Ops:
  6.5 0.9 convert_element_type.18
  7.4 0.1 mul.20
  7.5 1.8 %bitcast_multiply_fusion = bf16[256,4096]{1,0:T(8,128)(2,1)S(1)} fusion(bf16[1,16,16,4096]{3,2,1,0:T(8,128)(2,1)} %param.10, bf16[256]{0:T(256)(128)(2,1)S(1)} %mul.20), kind=kLoop, calls=%fused_computation.2 | loop fusion | flops 1048576 | bytes 4194816 | tf_op jit(solution)/shard_map/mul | solution.py:40
  9.3 1.3 %fusion.7 = f32[256,64]{0,1:T(8,128)S(1)} fusion(bf16[256,4096]{1,0:T(8,128)(2,1)S(1)} %bitcast_multiply_fusion, bf16[4096,128]{1,0:T(8,128)(2,1)S(1)} %bitcast.27), kind=kOutput, calls=%fused_computation.8 | convolution fusion | flops 134217728 | bytes 3211264 | tf_op jit(solution)/shard_map/dot_general | solution.py:17
  10.7 0.8 fusion.11
  11.6 3.7 %fusion.13 = f32[512,64]{0,1:T(8,128)S(1)} fusion(bf16[512,4096]{1,0:T(8,128)(2,1)} %bitcast.31, bf16[4096,128]{1,0:T(8,128)(2,1)S(1)} %bitcast.29), kind=kOutput, calls=%fused_computation.14 | convolution fusion | flops 268435456 | bytes 5373952 | tf_op jit(solution)/shard_map/dot_general | solution.py:12
  15.3 1.7 %fusion.9 = f32[512,64]{0,1:T(8,128)S(1)} fusion(bf16[512,4096]{1,0:T(8,128)(2,1)S(1)} %bitcast.32, bf16[4096,128]{1,0:T(8,128)(2,1)S(1)} %bitcast.30), kind=kOutput, calls=%fused_computation.10 | convolution fusion | flops 268435456 | bytes 5373952 | tf_op jit(solution)/shard_map/dot_general | solution.py:17
  17.1 0.2 reshape.24
  17.3 0.2 pad_maximum_fusion
  17.4 0.9 copy.10
  18.4 0.6 dynamic-slice
  19.7 27.3 %all-reduce.3.cloned.1.call-done = f32[768,128]{1,0:T(8,128)} async-done(((f32[768,128]{1,0:T(8,128)}), f32[768,128]{1,0:T(8,128)}) %all-reduce.3.cloned.1.call-update) | async-done | bytes 393232 | tf_op jit(solution)/shard_map/psum | solution.py:55
  47.0 0.8 constant_dynamic-slice_fusion.1
  47.8 0.7 fusion.3
  48.5 0.2 convert_element_type.22
  48.7 31.4 %all_gather.6 = bf16[64,4096]{1,0:T(8,128)(2,1)S(1)} all-gather(bf16[8,4096]{1,0:T(8,128)(2,1)S(1)} %convert_element_type.22), channel_id=1, replica_groups=mesh['groups'=2,'dp'=4,'tensor'=2,'layer'=2] {'dp','tensor'}, dimensions={0}, use_global_device_ids=true | all-gather | bytes 589824 | tf_op jit(solution)/shard_map/all_gather | solution.py:63
  80.1 3.0 %fusion.4 = bf16[64,512]{1,0:T(8,128)(2,1)S(1)} fusion(bf16[64,4096]{1,0:T(8,128)(2,1)S(1)} %all_gather.6, bf16[1,4096,512]{2,1,0:T(8,128)(2,1)} %param.13), kind=kOutput, calls=%fused_computation.7 | convolution fusion | flops 268468224 | bytes 4784128 | tf_op jit(solution)/shard_map/dot_general | solution.py:62
  83.2 31.2 %all_gather.7 = bf16[64,4096]{1,0:T(8,128)(2,1)S(1)} all-gather(bf16[64,512]{1,0:T(8,128)(2,1)S(1)} %fusion.4), channel_id=1, replica_groups=mesh['groups'=2,'dp'=4,'tensor'=2,'layer'=2] {'dp','tensor'}, dimensions={1}, use_global_device_ids=true | all-gather | bytes 589824 | tf_op jit(solution)/shard_map/all_gather | solution.py:69
  114.4 0.9 constant_dynamic-slice_fusion
  115.3 1.1 fusion.2
  116.4 0.3 convert_element_type.20
  116.7 0.2 fusion.19
  116.9 2.5 %all-reduce = f32[16,64]{1,0:T(8,128)S(1)} all-reduce(f32[16,64]{1,0:T(8,128)S(1)} %fusion.19), channel_id=2, replica_groups=mesh['groups'=2,'dp'=4,'tensor'=2,'layer'=2] {'layer'}, use_global_device_ids=true, to_apply=%region_1.0.clone | all-reduce | flops 1024 | bytes 8192
  119.4 0.6 dynamic-slice_multiply_fusion
  (13 shorter events, 0.1 us)
Async XLA Ops:
  6.5 4.2 %copy-start = (bf16[1,16,16,4096]{3,2,1,0:T(8,128)(2,1)S(1)}, bf16[1,16,16,4096]{3,2,1,0:T(8,128)(2,1)}, u32[]{:S(2)}) copy-start(bf16[1,16,16,4096]{3,2,1,0:T(8,128)(2,1)} %param.9) | copy-start | bytes 6291460
  6.5 2.8 %copy-start.1 = (bf16[1,4096,128]{2,1,0:T(8,128)(2,1)S(1)}, bf16[1,4096,128]{2,1,0:T(8,128)(2,1)}, u32[]{:S(2)}) copy-start(bf16[1,4096,128]{2,1,0:T(8,128)(2,1)} %param.12) | copy-start | bytes 3145732
  6.5 40.5 %all-reduce.3.cloned.1.call-start = ((), (), s32[]{:S(2)}) async-start(), calls=%async_computation | async-start | bytes 786432 | tf_op jit(solution)/shard_map/psum | solution.py:55
  11.6 3.7 %copy-start.2 = (bf16[1,32,16,4096]{3,2,1,0:T(8,128)(2,1)S(1)}, bf16[1,32,16,4096]{3,2,1,0:T(8,128)(2,1)}, u32[]{:S(2)}) copy-start(bf16[1,32,16,4096]{3,2,1,0:T(8,128)(2,1)} %param.8) | copy-start | bytes 12582916
  15.3 3.1 %copy-start.3 = (u32[32]{0:T(128)S(1)}, u32[32]{0:T(128)}, u32[]{:S(2)}) copy-start(u32[32]{0:T(128)} %constant.25) | copy-start | bytes 388
Sparse Core Ops, SparseCore 0:
  18.5 28.4 all-reduce.2
where the time goes:
time: 127 us
  blocking collectives  65.1 us (51%)
  waiting for transfers between devices  27.3 us (21%)
  between operations  14.2 us (11%)
  matrix products  12.6 us (10%)
  local copies, waits for them, and re-layouts  4.08 us (3%)
  other arithmetic  3.48 us (3%)
    all_gather x1, blocking collectives, local(): lax.all_gather(bench_feats, ('dp', 'tensor'), axis=0, tiled=True)  31.4 us
    all_gather x1, blocking collectives, local(): whole_pre = lax.all_gather(pre_cols, ('dp', 'tensor'), axis=1, tiled=True)  31.2 us
    psum x1, waiting for transfers between devices, local(): summed = lax.psum(blocks, 'tensor')  27.3 us
    dot_general x2, matrix products, project(): jnp.dot(inputs_here.reshape(examples * length, shard_width), factor[:, :f...  4.5 us
    dot_general x2, matrix products, project(): jnp.dot(grads_here.reshape(examples * length, shard_width), factor[:, fac...  3.09 us
    dot_general x1, matrix products, local(): jnp.dot(lax.all_gather(bench_feats, ('dp', 'tensor'), axis=0, tiled=True)...  3.02 us
  transfers between devices with their start and end apart: 1, of which 1 were waited for; matrix products, arithmetic and copies ran while one was open for 0% of the time, Pallas kernels for 0%

commit v1 on v0

--- a/solution.py
+++ b/solution.py
@@ -1,9 +1,14 @@
+import functools
 import math
 
 import jax
 import jax.numpy as jnp
 from jax import lax
+from jax.experimental import pallas as pl
+from jax.experimental.pallas import tpu as pltpu
 from jax.sharding import PartitionSpec as P
+
+MESH = pl.DeviceIdType.MESH
 
 
 def project(inputs_here, grads_here, factor):
@@ -74,6 +79,322 @@
     return scores * score_scale
 
 
+def fused_kernel(
+    dims,
+    ti, tg, bi, bg, mask, fac, pre,
+    out,
+    bench_v, train_v, fac_v, mask_v, pre_v,
+    bench_part, bench_recv, train_part, train_recv,
+    feats, train_f, t_send, t_all, partial_v, score_recv,
+    load_sem, swap_send, swap_recv, feat_send, feat_recv, fwd_send,
+    t_send_sem, t_recv_sem, score_send, score_recv_sem,
+):
+    n_dp, chunks, scale = dims
+    f32, bf16 = jnp.float32, jnp.bfloat16
+    z, x, layer = lax.axis_index("dp"), lax.axis_index("tensor"), lax.axis_index("layer")
+    other = 1 - x
+    slots = 2 * n_dp
+    me = z * 2 + x
+    bench_rows = bench_v.shape[2]
+    train_rows = train_v.shape[2]
+    length = mask.shape[1]
+    width = 64
+    chunk_width = feats.shape[3]
+    blocks_per_chunk = chunk_width // 128
+    columns = pre_v.shape[1]
+
+    def load(source, target, index):
+        return pltpu.make_async_copy(source, target, load_sem.at[index])
+
+    def half(ref, position, rows):
+        return ref.at[pl.ds(pl.multiple_of(position * rows, rows), rows), :]
+
+    fac_load = load(fac, fac_v, 0)
+    mask_load = load(mask, mask_v, 1)
+    bench_loads = [
+        load(half(ref, at, bench_rows), bench_v.at[h, i], 2 + 2 * h + i)
+        for h, at in enumerate((other, x)) for i, ref in enumerate((bi, bg))
+    ]
+    train_loads = [
+        load(half(ref, at, train_rows), train_v.at[h, i], 6 + 2 * h + i)
+        for h, at in enumerate((other, x)) for i, ref in enumerate((ti, tg))
+    ]
+    pre_load = load(pre, pre_v, 10)
+    fac_load.start()
+    for one in bench_loads:
+        one.start()
+    mask_load.start()
+    for one in train_loads:
+        one.start()
+    pre_load.start()
+
+    steps = [(dz, dx) for dz in range(n_dp) for dx in range(2)]
+    barrier = pltpu.get_barrier_semaphore()
+    for dz, dx in steps:
+        for dl in range(2):
+            if dz or dx or dl:
+                pl.semaphore_signal(
+                    barrier, inc=1,
+                    device_id={"dp": lax.rem(z + dz, n_dp), "tensor": lax.rem(x + dx, 2), "layer": lax.rem(layer + dl, 2)},
+                    device_id_type=MESH,
+                )
+
+    def project(ref, rows):
+        both = jnp.dot(
+            ref[...].reshape(2 * rows, ref.shape[2]), fac_v[...], preferred_element_type=f32
+        )
+        lane = lax.broadcasted_iota(jnp.int32, (rows, 128), 1)
+        return jnp.where(lane < width, both[:rows], both[rows:])
+
+    bench_swap = pltpu.make_async_remote_copy(
+        bench_part.at[0], bench_recv, swap_send.at[0], swap_recv.at[0],
+        device_id={"tensor": other}, device_id_type=MESH,
+    )
+    train_swap = pltpu.make_async_remote_copy(
+        train_part.at[0], train_recv, swap_send.at[1], swap_recv.at[1],
+        device_id={"tensor": other}, device_id_type=MESH,
+    )
+
+    fac_load.wait()
+    bench_loads[0].wait()
+    bench_loads[1].wait()
+    bench_part[0] = project(bench_v.at[0], bench_rows)
+    pl.semaphore_wait(barrier, 4 * n_dp - 1)
+    bench_swap.start()
+    bench_loads[2].wait()
+    bench_loads[3].wait()
+    bench_part[1] = project(bench_v.at[1], bench_rows)
+    train_loads[0].wait()
+    train_loads[1].wait()
+    train_part[0] = project(train_v.at[0], train_rows)
+    train_swap.start()
+
+    lane = lax.broadcasted_iota(jnp.int32, (8, 128), 1)
+
+    def token_rows(own, recv, base):
+        rows = []
+        for t in range(length):
+            window = pl.ds(base + t, 8, stride=length)
+            rows.append(own[window, :] + recv[window, :])
+        return rows
+
+    def doubled(row):
+        return jnp.where(lane < width, row, pltpu.roll(row, width, 1))
+
+    def outer_block(firsts, seconds, block):
+        index = width + 2 * block + jnp.where(lane < width, 0, 1)
+        total = None
+        for first, second in zip(firsts, seconds):
+            term = jnp.take_along_axis(first, index, axis=1, mode="promise_in_bounds") * second
+            total = term if total is None else total + term
+        return total * (1.0 / math.sqrt(length))
+
+    mask_load.wait()
+    bench_swap.wait_recv()
+    keep = mask_v[pl.ds(pl.multiple_of(x * 8, 8), 8), :].astype(f32)
+    rows = token_rows(bench_part.at[1], bench_recv, 0)
+    seconds = [doubled(row) for row in rows]
+    firsts = [row * keep[:, t : t + 1] for t, row in enumerate(rows)]
+
+    def feat_copy(c, slot, send_sem, device_id):
+        return pltpu.make_async_remote_copy(
+            feats.at[c, slot], feats.at[c, slot], send_sem, feat_recv.at[c, slot],
+            device_id=device_id, device_id_type=MESH,
+        )
+
+    sent = []
+    for c in range(chunks):
+        def bench_block(k, carry, c=c):
+            value = outer_block(firsts, seconds, c * blocks_per_chunk + k)
+            feats[c, me, :, pl.ds(pl.multiple_of(k * 128, 128), 128)] = value.astype(bf16)
+            return carry
+
+        lax.fori_loop(0, blocks_per_chunk, bench_block, 0)
+        for dz in range(1, n_dp):
+            sent.append(feat_copy(c, me, feat_send.at[c, dz], {"dp": lax.rem(z + dz, n_dp)}))
+        sent.append(feat_copy(c, me, feat_send.at[c, 0], {"tensor": other}))
+        for one in sent[-n_dp:]:
+            one.start()
+
+    train_loads[2].wait()
+    train_loads[3].wait()
+    train_part[1] = project(train_v.at[1], train_rows)
+
+    def forward(c):
+        for dz in range(1, n_dp):
+            slot = lax.rem(z + n_dp - dz, n_dp) * 2 + x
+            one = feat_copy(c, slot, fwd_send.at[c, dz], {"tensor": other})
+            one.wait_recv()
+            one.start()
+            sent.append(one)
+
+    forward(0)
+    forward(1)
+
+    train_swap.wait_recv()
+    per_slot = columns // 128
+    groups_of_8 = train_f.shape[1] // 8
+    for part in range(groups_of_8):
+        rows = token_rows(train_part.at[1], train_recv, part * 8 * length)
+        seconds_t = [doubled(row) for row in rows]
+
+        def train_block(block, carry, rows=rows, seconds_t=seconds_t, part=part):
+            train_f[block, part * 8 : part * 8 + 8, :] = outer_block(rows, seconds_t, block)
+            return carry
+
+        lax.fori_loop(0, slots * per_slot, train_block, 0)
+
+    def t_copy(r, dz, dx):
+        target = lax.rem(z + dz, n_dp) * 2 + lax.rem(x + dx, 2)
+        return pltpu.make_async_remote_copy(
+            t_send.at[target], t_all.at[r], t_send_sem.at[r], t_recv_sem.at[r],
+            device_id={"dp": lax.rem(z + dz, n_dp), "tensor": lax.rem(x + dx, 2)}, device_id_type=MESH,
+        )
+
+    def pack(slot, carry):
+        for k in range(per_slot):
+            t_send[slot, :, k * 128 : (k + 1) * 128] = train_f[slot * per_slot + k].astype(bf16)
+        return carry
+
+    lax.fori_loop(0, slots, pack, 0)
+    t_copies = [t_copy(r, dz, dx) for r, (dz, dx) in enumerate(steps) if r]
+    for one in t_copies:
+        one.start()
+    t_all[0] = t_send[me]
+
+    for c in range(2, chunks):
+        forward(c)
+
+    pre_load.wait()
+    total = None
+    for c in range(chunks):
+        for zz in range(n_dp):
+            slot = zz * 2 + other
+            feat_copy(c, slot, feat_send.at[c, 0], {"tensor": other}).wait_recv()
+        left = feats[c].astype(f32).reshape(slots * 8, chunk_width).astype(bf16)
+        term = jnp.dot(
+            left, pre_v[c * chunk_width : (c + 1) * chunk_width, :], preferred_element_type=f32
+        )
+        total = term if total is None else total + term
+    bench_pre = jnp.concatenate([total, jnp.zeros((128 - slots * 8, columns), f32)], axis=0).astype(bf16)
+
+    for one in t_copies:
+        one.wait_recv()
+    examples = t_all.shape[1]
+    scores = lax.dot_general(
+        t_all[...].reshape(slots * examples, columns), bench_pre,
+        (((1,), (1,)), ((), ())), preferred_element_type=f32,
+    )
+    partial_v[...] = scores.reshape(slots, 2, 8, 128)
+    score_copies = []
+    for r, (dz, dx) in enumerate(steps):
+        for dl in range(2):
+            if r or dl:
+                score_copies.append(
+                    pltpu.make_async_remote_copy(
+                        partial_v.at[r, lax.rem(layer + dl, 2)], score_recv.at[2 * r + dl],
+                        score_send.at[2 * r + dl], score_recv_sem.at[2 * r + dl],
+                        device_id={
+                            "dp": lax.rem(z + n_dp - dz, n_dp),
+                            "tensor": lax.rem(x + dx, 2),
+                            "layer": lax.rem(layer + dl, 2),
+                        },
+                        device_id_type=MESH,
+                    )
+                )
+    for one in score_copies:
+        one.start()
+    result = partial_v[0, layer]
+    for index, one in enumerate(score_copies):
+        one.wait_recv()
+        result = result + score_recv[index + 1]
+    out[...] = result[:, : out.shape[1]] * scale
+
+    bench_swap.wait_send()
+    train_swap.wait_send()
+    for one in sent + t_copies + score_copies:
+        one.wait_send()
+
+
+def fused(train_inputs, train_grads, bench_inputs, bench_grads, answer_mask, factors, precond):
+    f32, bf16 = jnp.float32, jnp.bfloat16
+    _, train, length, shard = train_inputs.shape
+    bench = bench_inputs.shape[1]
+    n_dp = lax.axis_size("dp")
+    slots = 2 * n_dp
+    features, columns = precond.shape[1:]
+    chunks = 4
+    scale = 1.0 / math.sqrt(features * lax.axis_size("layer"))
+    train_rows, bench_rows = train * length // 2, bench * length // 2
+    dma = pltpu.SemaphoreType.DMA
+    anywhere = pl.BlockSpec(memory_space=pl.ANY)
+    return pl.pallas_call(
+        functools.partial(fused_kernel, (n_dp, chunks, scale)),
+        out_shape=jax.ShapeDtypeStruct((8, slots * 8), f32),
+        in_specs=[anywhere] * 7,
+        out_specs=pl.BlockSpec(memory_space=pltpu.VMEM),
+        scratch_shapes=[
+            pltpu.VMEM((2, 2, bench_rows, shard), bf16),
+            pltpu.VMEM((2, 2, train_rows, shard), bf16),
+            pltpu.VMEM((shard, 128), bf16),
+            pltpu.VMEM((bench, length), jnp.int32),
+            pltpu.VMEM((features, columns), bf16),
+            pltpu.VMEM((2, bench_rows, 128), f32),
+            pltpu.VMEM((bench_rows, 128), f32),
+            pltpu.VMEM((2, train_rows, 128), f32),
+            pltpu.VMEM((train_rows, 128), f32),
+            pltpu.VMEM((chunks, slots, 8, features // chunks), bf16),
+            pltpu.VMEM((features // 128, train // 2, 128), f32),
+            pltpu.VMEM((slots, train // 2, columns), bf16),
+            pltpu.VMEM((slots, train // 2, columns), bf16),
+            pltpu.VMEM((slots, 2, 8, 128), f32),
+            pltpu.VMEM((2 * slots, 8, 128), f32),
+            dma((11,)),
+            dma((2,)),
+            dma((2,)),
+            dma((chunks, n_dp)),
+            dma((chunks, slots)),
+            dma((chunks, n_dp)),
+            dma((slots,)),
+            dma((slots,)),
+            dma((2 * slots,)),
+            dma((2 * slots,)),
+        ],
+        compiler_params=pltpu.CompilerParams(
+            collective_id=0, has_side_effects=True, vmem_limit_bytes=56 * 1024 * 1024
+        ),
+    )(
+        train_inputs.reshape(train * length, shard),
+        train_grads.reshape(train * length, shard),
+        bench_inputs.reshape(bench * length, shard),
+        bench_grads.reshape(bench * length, shard),
+        answer_mask,
+        factors[0],
+        precond[0],
+    )
+
+
+def fits(shapes, sizes):
+    train, bench, length, shard, half_width, features, columns, layers = shapes
+    n_dp, n_tensor, n_layer = sizes
+    return (
+        n_tensor == 2 and n_layer == 2 and layers == 1 and half_width == 64 and length == 16
+        and bench == 16 and train == 32 and n_dp * 16 <= 128
+        and shard % 256 == 0 and columns % 128 == 0 and features == 4096
+        and features == 2 * n_dp * columns
+    )
+
+
+def local_any(*args):
+    train_inputs, _, bench_inputs, _, _, factors, precond = args
+    shapes = (
+        train_inputs.shape[1], bench_inputs.shape[1], train_inputs.shape[2], train_inputs.shape[3],
+        factors.shape[2] // 2, precond.shape[1], precond.shape[2], train_inputs.shape[0],
+    )
+    sizes = tuple(lax.axis_size(name) for name in ("dp", "tensor", "layer"))
+    return fused(*args) if fits(shapes, sizes) else local(*args)
+
+
 def solution(mesh):
     placed = (
         P("layer", ("groups", "dp"), None, "tensor"),
@@ -85,7 +406,7 @@
         P("layer", None, ("dp", "tensor")),
     )
     return jax.shard_map(
-        local,
+        local_any,
         mesh=mesh,
         in_specs=placed,
         out_specs=P(("groups", "dp", "tensor", "layer"), None),

time: 127 us -> 35.2 us (0.28)
  blocking collectives: 65.1 us -> 0 us
  Pallas kernels: 0 us -> 33.7 us
  waiting for transfers between devices: 27.3 us -> 0 us
  between operations: 14.2 us -> 0.01 us
  matrix products: 12.6 us -> 0 us
  other arithmetic: 3.48 us -> 0 us
  local copies, waits for them, and re-layouts: 4.08 us -> 1.28 us
    all_gather x2 -> x0, blocking collectives: 62.6 us -> none  [the longest x1 31.4 us: local(): lax.all_gather(bench_feats, ('dp', 'tensor'), axis=0, tiled=True)]
    pallas_call x0 -> x1, Pallas kernels: none -> 33.7 us  [fused(): pl.pallas_call(functools.partial(fused_kernel, (n_dp, chunks, scale)), ou...]
    psum x1 -> x0, waiting for transfers between devices: 27.3 us -> none  [local(): summed = lax.psum(blocks, 'tensor')]
    dot_general x8 -> x0, matrix products: 12.6 us -> none  [the longest x2 4.5 us: project(): jnp.dot(inputs_here.reshape(examples * length, shard_width), factor[:, :f...]
    unnamed x1 -> x0, blocking collectives: 2.48 us -> none
    mul x2 -> x0, other arithmetic: 2.42 us -> none  [the longest x1 1.83 us: local(): masked = bench_grads[0] * answer_mask.astype(jnp.bfloat16)[:, :, None]]
    slice x2 -> x0, local copies, waits for them, and re-layouts: 1.76 us -> none  [the longest x1 0.91 us: local(): own_rows[:train_each * length]]
  transfers between devices with their start and end apart: 1 -> 0, of which waited for: 1 -> 0; matrix products, arithmetic and copies ran while one was open for 0% -> 0% of each run, Pallas kernels for 0% -> 0%
where the time goes in v1:
time: 35.2 us; the launch traced here: 35 us
  Pallas kernels  33.7 us (96%)
  local copies, waits for them, and re-layouts  1.28 us (4%)
    pallas_call x1, Pallas kernels, fused(): pl.pallas_call(functools.partial(fused_kernel, (n_dp, chunks, scale)), ou...  33.7 us
    unnamed x1, local copies, waits for them, and re-layouts  1.28 us

profile of v1, /device:TPU:0, one launch (start us, length us, event | category | flops | bytes accessed | tf_op | source)
XLA Modules:
  0.0 35.0 jit_solution(2997165465763314491)
XLA Ops:
  0.0 33.7 %shard_map.73 = f32[8,64]{1,0:T(8,128)} custom-call(bf16[512,4096]{1,0:T(8,128)(2,1)} %bitcast.6, bf16[512,4096]{1,0:T(8,128)(2,1)} %bitcast.7, bf16[256,4096]{1,0:T(8,128)(2,1)} %bitcast.9, bf16[256,4096]{1,0:T(8,128)(2,1)} %bitcast.10, s32[16,16]{1,0:T(8,128)} %mask.1, bf16[4096,128]{1,0:T(8,128)(2,1)} %bitcast.11, bf16[4096,512]{1,0:T(8,128)(2,1)} %bitcast.8), custom_call_target="tpu_custom_call" | custom-call | tf_op jit(solution)/shard_map/pallas_call | solution.py:331
  33.8 1.3 %copy.9 = f32[8,64]{1,0:T(8,128)} copy(f32[8,64]{1,0:T(8,128)} %shard_map.73) | data formatting | bytes 4096

commit v2 on v1

--- a/solution.py
+++ b/solution.py
@@ -85,7 +85,7 @@
     out,
     bench_v, train_v, fac_v, mask_v, pre_v,
     bench_part, bench_recv, train_part, train_recv,
-    feats, train_f, t_send, t_all, partial_v, score_recv,
+    feats, spread_v, t_send, t_all, partial_v, score_recv,
     load_sem, swap_send, swap_recv, feat_send, feat_recv, fwd_send,
     t_send_sem, t_recv_sem, score_send, score_recv_sem,
 ):
@@ -100,7 +100,7 @@
     length = mask.shape[1]
     width = 64
     chunk_width = feats.shape[3]
-    blocks_per_chunk = chunk_width // 128
+    span = 512
     columns = pre_v.shape[1]
 
     def load(source, target, index):
@@ -139,6 +139,15 @@
                     device_id_type=MESH,
                 )
 
+    def build(k, carry):
+        row = lax.broadcasted_iota(jnp.int32, (256, 256), 0)
+        column = lax.broadcasted_iota(jnp.int32, (256, 256), 1) + k * 256
+        hit = (row % 128) * width - width * width == column - column % width
+        spread_v[:, pl.ds(pl.multiple_of(k * 256, 256), 256)] = jnp.where(hit, 1.0, 0.0).astype(bf16)
+        return carry
+
+    lax.fori_loop(0, spread_v.shape[1] // 256, build, 0)
+
     def project(ref, rows):
         both = jnp.dot(
             ref[...].reshape(2 * rows, ref.shape[2]), fac_v[...], preferred_element_type=f32
@@ -181,20 +190,34 @@
     def doubled(row):
         return jnp.where(lane < width, row, pltpu.roll(row, width, 1))
 
-    def outer_block(firsts, seconds, block):
-        index = width + 2 * block + jnp.where(lane < width, 0, 1)
-        total = None
-        for first, second in zip(firsts, seconds):
-            term = jnp.take_along_axis(first, index, axis=1, mode="promise_in_bounds") * second
-            total = term if total is None else total + term
-        return total * (1.0 / math.sqrt(length))
+    def split(rows):
+        whole = jnp.concatenate(rows, axis=0)
+        high = whole.astype(bf16)
+        low = (whole - high.astype(f32)).astype(bf16)
+        return jnp.concatenate([high, low], axis=1)
+
+    def outer(parts, seconds, start, span):
+        spread = jnp.dot(
+            parts, spread_v[:, pl.ds(pl.multiple_of(start, span), span)], preferred_element_type=f32
+        )
+        values = []
+        for first in range(0, len(seconds), length):
+            lanes = []
+            for j in range(0, span, 128):
+                total = None
+                for t in range(first, first + length):
+                    term = spread[t * 8 : t * 8 + 8, j : j + 128] * seconds[t]
+                    total = term if total is None else total + term
+                lanes.append(total)
+            values.append(jnp.concatenate(lanes, axis=1))
+        return jnp.concatenate(values, axis=0) * (1.0 / math.sqrt(length))
 
     mask_load.wait()
     bench_swap.wait_recv()
     keep = mask_v[pl.ds(pl.multiple_of(x * 8, 8), 8), :].astype(f32)
     rows = token_rows(bench_part.at[1], bench_recv, 0)
     seconds = [doubled(row) for row in rows]
-    firsts = [row * keep[:, t : t + 1] for t, row in enumerate(rows)]
+    bench_split = split([row * keep[:, t : t + 1] for t, row in enumerate(rows)])
 
     def feat_copy(c, slot, send_sem, device_id):
         return pltpu.make_async_remote_copy(
@@ -205,11 +228,11 @@
     sent = []
     for c in range(chunks):
         def bench_block(k, carry, c=c):
-            value = outer_block(firsts, seconds, c * blocks_per_chunk + k)
-            feats[c, me, :, pl.ds(pl.multiple_of(k * 128, 128), 128)] = value.astype(bf16)
+            value = outer(bench_split, seconds, c * chunk_width + k * span, span)
+            feats[c, me, :, pl.ds(pl.multiple_of(k * span, span), span)] = value.astype(bf16)
             return carry
 
-        lax.fori_loop(0, blocks_per_chunk, bench_block, 0)
+        lax.fori_loop(0, chunk_width // span, bench_block, 0)
         for dz in range(1, n_dp):
             sent.append(feat_copy(c, me, feat_send.at[c, dz], {"dp": lax.rem(z + dz, n_dp)}))
         sent.append(feat_copy(c, me, feat_send.at[c, 0], {"tensor": other}))
@@ -232,17 +255,17 @@
     forward(1)
 
     train_swap.wait_recv()
-    per_slot = columns // 128
-    groups_of_8 = train_f.shape[1] // 8
-    for part in range(groups_of_8):
-        rows = token_rows(train_part.at[1], train_recv, part * 8 * length)
-        seconds_t = [doubled(row) for row in rows]
-
-        def train_block(block, carry, rows=rows, seconds_t=seconds_t, part=part):
-            train_f[block, part * 8 : part * 8 + 8, :] = outer_block(rows, seconds_t, block)
-            return carry
-
-        lax.fori_loop(0, slots * per_slot, train_block, 0)
+    rows = []
+    for part in range(0, t_send.shape[1], 8):
+        rows += token_rows(train_part.at[1], train_recv, part * length)
+    train_seconds = [doubled(row) for row in rows]
+    train_split = split(rows)
+
+    def train_block(slot, carry):
+        t_send[slot] = outer(train_split, train_seconds, slot * columns, columns).astype(bf16)
+        return carry
+
+    lax.fori_loop(0, slots, train_block, 0)
 
     def t_copy(r, dz, dx):
         target = lax.rem(z + dz, n_dp) * 2 + lax.rem(x + dx, 2)
@@ -251,12 +274,6 @@
             device_id={"dp": lax.rem(z + dz, n_dp), "tensor": lax.rem(x + dx, 2)}, device_id_type=MESH,
         )
 
-    def pack(slot, carry):
-        for k in range(per_slot):
-            t_send[slot, :, k * 128 : (k + 1) * 128] = train_f[slot * per_slot + k].astype(bf16)
-        return carry
-
-    lax.fori_loop(0, slots, pack, 0)
     t_copies = [t_copy(r, dz, dx) for r, (dz, dx) in enumerate(steps) if r]
     for one in t_copies:
         one.start()
@@ -344,7 +361,7 @@
             pltpu.VMEM((2, train_rows, 128), f32),
             pltpu.VMEM((train_rows, 128), f32),
             pltpu.VMEM((chunks, slots, 8, features // chunks), bf16),
-            pltpu.VMEM((features // 128, train // 2, 128), f32),
+            pltpu.VMEM((256, features), bf16),
             pltpu.VMEM((slots, train // 2, columns), bf16),
             pltpu.VMEM((slots, train // 2, columns), bf16),
             pltpu.VMEM((slots, 2, 8, 128), f32),

time: 35.2 us -> 30.1 us (0.86)
  Pallas kernels: 33.7 us -> 28.7 us
    pallas_call x1, Pallas kernels: 33.7 us -> 28.7 us  [fused(): pl.pallas_call(functools.partial(fused_kernel, (n_dp, chunks, scale)), ou...]
where the time goes in v2:
time: 30.1 us; the launch traced here: 30 us
  Pallas kernels  28.7 us (95%)
  local copies, waits for them, and re-layouts  1.28 us (4%)
    pallas_call x1, Pallas kernels, fused(): pl.pallas_call(functools.partial(fused_kernel, (n_dp, chunks, scale)), ou...  28.7 us
    unnamed x1, local copies, waits for them, and re-layouts  1.28 us

profile of v2, /device:TPU:0, one launch (start us, length us, event | category | flops | bytes accessed | tf_op | source)
XLA Modules:
  0.0 30.0 jit_solution(18068326125391379945)
XLA Ops:
  0.0 28.7 %shard_map.73 = f32[8,64]{1,0:T(8,128)} custom-call(bf16[512,4096]{1,0:T(8,128)(2,1)} %bitcast.6, bf16[512,4096]{1,0:T(8,128)(2,1)} %bitcast.7, bf16[256,4096]{1,0:T(8,128)(2,1)} %bitcast.9, bf16[256,4096]{1,0:T(8,128)(2,1)} %bitcast.10, s32[16,16]{1,0:T(8,128)} %mask.1, bf16[4096,128]{1,0:T(8,128)(2,1)} %bitcast.11, bf16[4096,512]{1,0:T(8,128)(2,1)} %bitcast.8), custom_call_target="tpu_custom_call" | custom-call | tf_op jit(solution)/shard_map/pallas_call | solution.py:348
  28.7 1.3 %copy.9 = f32[8,64]{1,0:T(8,128)} copy(f32[8,64]{1,0:T(8,128)} %shard_map.73) | data formatting | bytes 4096

commit v3 on v2

--- a/solution.py
+++ b/solution.py
@@ -85,11 +85,11 @@
     out,
     bench_v, train_v, fac_v, mask_v, pre_v,
     bench_part, bench_recv, train_part, train_recv,
-    feats, spread_v, t_send, t_all, partial_v, score_recv,
+    feats, proj, spread_v, t_send, t_all, partial_v, both_v, pair_recv, score_recv,
     load_sem, swap_send, swap_recv, feat_send, feat_recv, fwd_send,
     t_send_sem, t_recv_sem, score_send, score_recv_sem,
 ):
-    n_dp, chunks, scale = dims
+    n_dp, scale = dims
     f32, bf16 = jnp.float32, jnp.bfloat16
     z, x, layer = lax.axis_index("dp"), lax.axis_index("tensor"), lax.axis_index("layer")
     other = 1 - x
@@ -99,7 +99,6 @@
     train_rows = train_v.shape[2]
     length = mask.shape[1]
     width = 64
-    chunk_width = feats.shape[3]
     span = 512
     columns = pre_v.shape[1]
 
@@ -130,14 +129,12 @@
 
     steps = [(dz, dx) for dz in range(n_dp) for dx in range(2)]
     barrier = pltpu.get_barrier_semaphore()
-    for dz, dx in steps:
-        for dl in range(2):
-            if dz or dx or dl:
-                pl.semaphore_signal(
-                    barrier, inc=1,
-                    device_id={"dp": lax.rem(z + dz, n_dp), "tensor": lax.rem(x + dx, 2), "layer": lax.rem(layer + dl, 2)},
-                    device_id_type=MESH,
-                )
+    partners = [
+        {"dp": lax.rem(z + dz, n_dp), "tensor": lax.rem(x + dx, 2)} for dz, dx in steps if dz or dx
+    ]
+    partners.append({"layer": 1 - layer})
+    for partner in partners:
+        pl.semaphore_signal(barrier, inc=1, device_id=partner, device_id_type=MESH)
 
     def build(k, carry):
         row = lax.broadcasted_iota(jnp.int32, (256, 256), 0)
@@ -168,7 +165,7 @@
     bench_loads[0].wait()
     bench_loads[1].wait()
     bench_part[0] = project(bench_v.at[0], bench_rows)
-    pl.semaphore_wait(barrier, 4 * n_dp - 1)
+    pl.semaphore_wait(barrier, slots)
     bench_swap.start()
     bench_loads[2].wait()
     bench_loads[3].wait()
@@ -198,7 +195,7 @@
 
     def outer(parts, seconds, start, span):
         spread = jnp.dot(
-            parts, spread_v[:, pl.ds(pl.multiple_of(start, span), span)], preferred_element_type=f32
+            parts, spread_v[: parts.shape[1], pl.ds(pl.multiple_of(start, span), span)], preferred_element_type=f32
         )
         values = []
         for first in range(0, len(seconds), length):
@@ -217,42 +214,29 @@
     keep = mask_v[pl.ds(pl.multiple_of(x * 8, 8), 8), :].astype(f32)
     rows = token_rows(bench_part.at[1], bench_recv, 0)
     seconds = [doubled(row) for row in rows]
-    bench_split = split([row * keep[:, t : t + 1] for t, row in enumerate(rows)])
-
-    def feat_copy(c, slot, send_sem, device_id):
+    masked = [jnp.where(lane < width, row, row * keep[:, t : t + 1]) for t, row in enumerate(rows)]
+    proj[me] = jnp.concatenate(masked, axis=0).astype(bf16)
+
+    def proj_copy(slot, send_sem, device_id):
         return pltpu.make_async_remote_copy(
-            feats.at[c, slot], feats.at[c, slot], send_sem, feat_recv.at[c, slot],
+            proj.at[slot], proj.at[slot], send_sem, feat_recv.at[slot],
             device_id=device_id, device_id_type=MESH,
         )
 
-    sent = []
-    for c in range(chunks):
-        def bench_block(k, carry, c=c):
-            value = outer(bench_split, seconds, c * chunk_width + k * span, span)
-            feats[c, me, :, pl.ds(pl.multiple_of(k * span, span), span)] = value.astype(bf16)
-            return carry
-
-        lax.fori_loop(0, chunk_width // span, bench_block, 0)
-        for dz in range(1, n_dp):
-            sent.append(feat_copy(c, me, feat_send.at[c, dz], {"dp": lax.rem(z + dz, n_dp)}))
-        sent.append(feat_copy(c, me, feat_send.at[c, 0], {"tensor": other}))
-        for one in sent[-n_dp:]:
-            one.start()
+    sent = [proj_copy(me, feat_send.at[dz], {"dp": lax.rem(z + dz, n_dp)}) for dz in range(1, n_dp)]
+    sent.append(proj_copy(me, feat_send.at[0], {"tensor": other}))
+    for one in sent:
+        one.start()
 
     train_loads[2].wait()
     train_loads[3].wait()
     train_part[1] = project(train_v.at[1], train_rows)
 
-    def forward(c):
-        for dz in range(1, n_dp):
-            slot = lax.rem(z + n_dp - dz, n_dp) * 2 + x
-            one = feat_copy(c, slot, fwd_send.at[c, dz], {"tensor": other})
-            one.wait_recv()
-            one.start()
-            sent.append(one)
-
-    forward(0)
-    forward(1)
+    for dz in range(1, n_dp):
+        one = proj_copy(lax.rem(z + n_dp - dz, n_dp) * 2 + x, fwd_send.at[dz], {"tensor": other})
+        one.wait_recv()
+        one.start()
+        sent.append(one)
 
     train_swap.wait_recv()
     rows = []
@@ -265,7 +249,7 @@
         t_send[slot] = outer(train_split, train_seconds, slot * columns, columns).astype(bf16)
         return carry
 
-    lax.fori_loop(0, slots, train_block, 0)
+    lax.fori_loop(0, slots, train_block, 0, unroll=4)
 
     def t_copy(r, dz, dx):
         target = lax.rem(z + dz, n_dp) * 2 + lax.rem(x + dx, 2)
@@ -279,54 +263,75 @@
         one.start()
     t_all[0] = t_send[me]
 
-    for c in range(2, chunks):
-        forward(c)
+    def bench_slot(slot):
+        tokens = proj[slot]
+        bench_seconds = [doubled(tokens[t * 8 : t * 8 + 8].astype(f32)) for t in range(length)]
+
+        def bench_block(k, carry):
+            start = pl.multiple_of(k * span, span)
+            feats[slot, :, pl.ds(start, span)] = outer(tokens, bench_seconds, start, span)
+            return carry
+
+        lax.fori_loop(0, feats.shape[2] // span, bench_block, 0, unroll=True)
+
+    def own_column(dz, carry):
+        bench_slot(lax.rem(z + n_dp - dz, n_dp) * 2 + x)
+        return carry
+
+    lax.fori_loop(0, n_dp, own_column, 0)
+
+    def other_column(dz, carry):
+        slot = lax.rem(z + n_dp - dz, n_dp) * 2 + other
+        proj_copy(slot, feat_send.at[0], {"tensor": other}).wait_recv()
+        bench_slot(slot)
+        return carry
+
+    lax.fori_loop(0, n_dp, other_column, 0)
 
     pre_load.wait()
-    total = None
-    for c in range(chunks):
-        for zz in range(n_dp):
-            slot = zz * 2 + other
-            feat_copy(c, slot, feat_send.at[c, 0], {"tensor": other}).wait_recv()
-        left = feats[c].astype(f32).reshape(slots * 8, chunk_width).astype(bf16)
-        term = jnp.dot(
-            left, pre_v[c * chunk_width : (c + 1) * chunk_width, :], preferred_element_type=f32
-        )
-        total = term if total is None else total + term
-    bench_pre = jnp.concatenate([total, jnp.zeros((128 - slots * 8, columns), f32)], axis=0).astype(bf16)
+    total = jnp.dot(
+        feats[...].reshape(slots * 8, feats.shape[2]).astype(bf16), pre_v[...], preferred_element_type=f32
+    )
+    bench_pre = jnp.concatenate([total, jnp.zeros((128 - slots * 8, columns), f32)], axis=0)
+    pre_high = bench_pre.astype(bf16)
+    pre_low = (bench_pre - pre_high.astype(f32)).astype(bf16)
 
     for one in t_copies:
         one.wait_recv()
     examples = t_all.shape[1]
-    scores = lax.dot_general(
-        t_all[...].reshape(slots * examples, columns), bench_pre,
-        (((1,), (1,)), ((), ())), preferred_element_type=f32,
-    )
-    partial_v[...] = scores.reshape(slots, 2, 8, 128)
+    held = t_all[...].reshape(slots * examples, columns)
+    along = (((1,), (1,)), ((), ()))
+    scores = lax.dot_general(held, pre_high, along, preferred_element_type=f32)
+    scores += lax.dot_general(held, pre_low, along, preferred_element_type=f32)
+    scores = scores.reshape(slots, 2, 8, 128)
+    for which in range(2):
+        partial_v[which] = scores[:, which]
+    pair = pltpu.make_async_remote_copy(
+        partial_v.at[1 - layer], pair_recv, score_send.at[0], score_recv_sem.at[0],
+        device_id={"layer": 1 - layer}, device_id_type=MESH,
+    )
+    pair.start()
+    pair.wait_recv()
+    both_v[...] = partial_v[layer] + pair_recv[...]
     score_copies = []
     for r, (dz, dx) in enumerate(steps):
-        for dl in range(2):
-            if r or dl:
-                score_copies.append(
-                    pltpu.make_async_remote_copy(
-                        partial_v.at[r, lax.rem(layer + dl, 2)], score_recv.at[2 * r + dl],
-                        score_send.at[2 * r + dl], score_recv_sem.at[2 * r + dl],
-                        device_id={
-                            "dp": lax.rem(z + n_dp - dz, n_dp),
-                            "tensor": lax.rem(x + dx, 2),
-                            "layer": lax.rem(layer + dl, 2),
-                        },
-                        device_id_type=MESH,
-                    )
+        if r:
+            score_copies.append(
+                pltpu.make_async_remote_copy(
+                    both_v.at[r], score_recv.at[r], score_send.at[r], score_recv_sem.at[r],
+                    device_id={"dp": lax.rem(z + n_dp - dz, n_dp), "tensor": lax.rem(x + dx, 2)},
+                    device_id_type=MESH,
                 )
+            )
     for one in score_copies:
         one.start()
-    result = partial_v[0, layer]
+    result = both_v[0]
     for index, one in enumerate(score_copies):
         one.wait_recv()
         result = result + score_recv[index + 1]
     out[...] = result[:, : out.shape[1]] * scale
 
+    pair.wait_send()
     bench_swap.wait_send()
     train_swap.wait_send()
     for one in sent + t_copies + score_copies:
@@ -340,13 +345,12 @@
     n_dp = lax.axis_size("dp")
     slots = 2 * n_dp
     features, columns = precond.shape[1:]
-    chunks = 4
     scale = 1.0 / math.sqrt(features * lax.axis_size("layer"))
     train_rows, bench_rows = train * length // 2, bench * length // 2
     dma = pltpu.SemaphoreType.DMA
     anywhere = pl.BlockSpec(memory_space=pl.ANY)
     return pl.pallas_call(
-        functools.partial(fused_kernel, (n_dp, chunks, scale)),
+        functools.partial(fused_kernel, (n_dp, scale)),
         out_shape=jax.ShapeDtypeStruct((8, slots * 8), f32),
         in_specs=[anywhere] * 7,
         out_specs=pl.BlockSpec(memory_space=pltpu.VMEM),
@@ -360,22 +364,25 @@
             pltpu.VMEM((bench_rows, 128), f32),
             pltpu.VMEM((2, train_rows, 128), f32),
             pltpu.VMEM((train_rows, 128), f32),
-            pltpu.VMEM((chunks, slots, 8, features // chunks), bf16),
+            pltpu.VMEM((slots, 8, features), f32),
+            pltpu.VMEM((slots, bench_rows, 128), bf16),
             pltpu.VMEM((256, features), bf16),
             pltpu.VMEM((slots, train // 2, columns), bf16),
             pltpu.VMEM((slots, train // 2, columns), bf16),
-            pltpu.VMEM((slots, 2, 8, 128), f32),
-            pltpu.VMEM((2 * slots, 8, 128), f32),
+            pltpu.VMEM((2, slots, 8, 128), f32),
+            pltpu.VMEM((slots, 8, 128), f32),
+            pltpu.VMEM((slots, 8, 128), f32),
+            pltpu.VMEM((slots, 8, 128), f32),
             dma((11,)),
             dma((2,)),
             dma((2,)),
-            dma((chunks, n_dp)),
-            dma((chunks, slots)),
-            dma((chunks, n_dp)),
+            dma((n_dp,)),
+            dma((slots,)),
+            dma((n_dp,)),
             dma((slots,)),
             dma((slots,)),
-            dma((2 * slots,)),
-            dma((2 * slots,)),
+            dma((slots,)),
+            dma((slots,)),
         ],
         compiler_params=pltpu.CompilerParams(
             collective_id=0, has_side_effects=True, vmem_limit_bytes=56 * 1024 * 1024

time: 30.1 us -> 27.1 us (0.900)
  Pallas kernels: 28.7 us -> 25.6 us
    pallas_call x1, Pallas kernels: 28.7 us -> 25.6 us  [fused(): pl.pallas_call(functools.partial(fused_kernel, (n_dp, scale)), out_shape=...]
where the time goes in v3:
time: 27.1 us; the launch traced here: 26.9 us
  Pallas kernels  25.6 us (94%)
  local copies, waits for them, and re-layouts  1.28 us (5%)
    pallas_call x1, Pallas kernels, fused(): pl.pallas_call(functools.partial(fused_kernel, (n_dp, scale)), out_shape=...  25.6 us
    unnamed x1, local copies, waits for them, and re-layouts  1.28 us

profile of v3, /device:TPU:0, one launch (start us, length us, event | category | flops | bytes accessed | tf_op | source)
XLA Modules:
  0.0 26.9 jit_solution(6779751716608165832)
XLA Ops:
  0.0 25.6 %shard_map.73 = f32[8,64]{1,0:T(8,128)} custom-call(bf16[512,4096]{1,0:T(8,128)(2,1)} %bitcast.6, bf16[512,4096]{1,0:T(8,128)(2,1)} %bitcast.7, bf16[256,4096]{1,0:T(8,128)(2,1)} %bitcast.9, bf16[256,4096]{1,0:T(8,128)(2,1)} %bitcast.10, s32[16,16]{1,0:T(8,128)} %mask.1, bf16[4096,128]{1,0:T(8,128)(2,1)} %bitcast.11, bf16[4096,512]{1,0:T(8,128)(2,1)} %bitcast.8), custom_call_target="tpu_custom_call" | custom-call | tf_op jit(solution)/shard_map/pallas_call | solution.py:352
  25.6 1.3 %copy.9 = f32[8,64]{1,0:T(8,128)} copy(f32[8,64]{1,0:T(8,128)} %shard_map.73) | data formatting | bytes 4096

commit v4 on v3

--- a/solution.py
+++ b/solution.py
@@ -232,6 +232,19 @@
     train_loads[3].wait()
     train_part[1] = project(train_v.at[1], train_rows)
 
+    def bench_slot(slot):
+        tokens = proj[slot]
+        bench_seconds = [doubled(tokens[t * 8 : t * 8 + 8].astype(f32)) for t in range(length)]
+
+        def bench_block(k, carry):
+            start = pl.multiple_of(k * span, span)
+            feats[slot, :, pl.ds(start, span)] = outer(tokens, bench_seconds, start, span)
+            return carry
+
+        lax.fori_loop(0, feats.shape[2] // span, bench_block, 0, unroll=True)
+
+    bench_slot(me)
+
     for dz in range(1, n_dp):
         one = proj_copy(lax.rem(z + n_dp - dz, n_dp) * 2 + x, fwd_send.at[dz], {"tensor": other})
         one.wait_recv()
@@ -263,22 +276,11 @@
         one.start()
     t_all[0] = t_send[me]
 
-    def bench_slot(slot):
-        tokens = proj[slot]
-        bench_seconds = [doubled(tokens[t * 8 : t * 8 + 8].astype(f32)) for t in range(length)]
-
-        def bench_block(k, carry):
-            start = pl.multiple_of(k * span, span)
-            feats[slot, :, pl.ds(start, span)] = outer(tokens, bench_seconds, start, span)
-            return carry
-
-        lax.fori_loop(0, feats.shape[2] // span, bench_block, 0, unroll=True)
-
     def own_column(dz, carry):
         bench_slot(lax.rem(z + n_dp - dz, n_dp) * 2 + x)
         return carry
 
-    lax.fori_loop(0, n_dp, own_column, 0)
+    lax.fori_loop(1, n_dp, own_column, 0)
 
     def other_column(dz, carry):
         slot = lax.rem(z + n_dp - dz, n_dp) * 2 + other

time: 27.1 us -> 26.8 us (0.989)
  Pallas kernels: 25.6 us -> 25.3 us
    pallas_call x1, Pallas kernels: 25.6 us -> 25.3 us  [fused(): pl.pallas_call(functools.partial(fused_kernel, (n_dp, scale)), out_shape=...]
where the time goes in v4:
time: 26.8 us; the launch traced here: 26.6 us
  Pallas kernels  25.3 us (94%)
  local copies, waits for them, and re-layouts  1.28 us (5%)
    pallas_call x1, Pallas kernels, fused(): pl.pallas_call(functools.partial(fused_kernel, (n_dp, scale)), out_shape=...  25.3 us
    unnamed x1, local copies, waits for them, and re-layouts  1.28 us

profile of v4, /device:TPU:0, one launch (start us, length us, event | category | flops | bytes accessed | tf_op | source)
XLA Modules:
  0.0 26.6 jit_solution(6894028393672651001)
XLA Ops:
  0.0 25.3 %shard_map.73 = f32[8,64]{1,0:T(8,128)} custom-call(bf16[512,4096]{1,0:T(8,128)(2,1)} %bitcast.6, bf16[512,4096]{1,0:T(8,128)(2,1)} %bitcast.7, bf16[256,4096]{1,0:T(8,128)(2,1)} %bitcast.9, bf16[256,4096]{1,0:T(8,128)(2,1)} %bitcast.10, s32[16,16]{1,0:T(8,128)} %mask.1, bf16[4096,128]{1,0:T(8,128)(2,1)} %bitcast.11, bf16[4096,512]{1,0:T(8,128)(2,1)} %bitcast.8), custom_call_target="tpu_custom_call" | custom-call | tf_op jit(solution)/shard_map/pallas_call | solution.py:354
  25.4 1.3 %copy.9 = f32[8,64]{1,0:T(8,128)} copy(f32[8,64]{1,0:T(8,128)} %shard_map.73) | data formatting | bytes 4096
